TPU v7x, 256 devices: a whole 4x4x8 slice. The times are simulated.
256 devices in a mesh: gx: 64 (over z, y, x_hi), gy: 4 (over x_lo, core).
Axes of the slice: x: 4 (x_hi: 2, x_lo: 2; x = x_hi * 2 + x_lo), y: 4, z: 8, core: 2. Of those that a mesh axis runs over, the one named last changes fastest.
Arguments:
- points: bfloat16 [4, 64, 64, 32, 128], P('gy', 'gx'), may hold values from -6 to 6
- counts: int32 [4, 64, 64], P('gy', 'gx'), may hold values from 10 to 32, as said below
- voxels: int32 [4, 64, 64, 32], P('gy', 'gx'), may hold values from 0 to 1023, as said below
- occupancy: int32 [64, 4, 2], P('gx', 'gy'), may hold values from 0 to 1, as said below
- weight: bfloat16 [27, 96, 96], replicated, may hold values from -0.125 to 0.125
- w_in: bfloat16 [128, 96], replicated, may hold values from -0.5 to 0.5
- cotangent: bfloat16 [512, 32, 16, 96], P('gx', 'gy'), may hold values from -6 to 6
Outputs:
- point_feat: bfloat16 [4, 64, 64, 32, 96], P('gy', 'gx')
- point_grad: bfloat16 [4, 64, 64, 32, 128], P('gy', 'gx')
- weight_grad: float32 [27, 96, 96], replicated
Inputs may be any that keep to these rules, and one draw needn't show every extreme that they name: `counts`: in each gy row one owner receives 32 rows from every source. `voxels`: every slot's voxel lies in an occupied block of its owner tile. `occupancy`: every tile has at least one occupied block.
All inputs are finite; a program needn't handle non-finite values.
Results may differ from a plain program's by a relative error of at most 0.01.
Values may be sent and summed in bfloat16 or wider, within the bound.
A program may use at most 64 MiB of HBM per device.

v0:
```python
import jax
import jax.numpy as jnp
from jax import lax
from jax.sharding import PartitionSpec as P


def padded_2(block, sides, width):
    for axis, dim in sides:
        count = lax.axis_size(axis)
        forward = [(i, i + 1) for i in range(count - 1)]
        backward = [(target, source) for source, target in forward]
        low = lax.ppermute(
            lax.slice_in_dim(block, block.shape[dim] - width, None, axis=dim), axis, forward
        )
        high = lax.ppermute(lax.slice_in_dim(block, 0, width, axis=dim), axis, backward)
        block = jnp.concatenate([low, block, high], axis=dim)
    return block


def pad_depth(field):
    return jnp.pad(field, ((0, 0), (0, 0), (1, 1), (0, 0)))


def forward_taps(padded, weight, depth, width):
    total = jnp.zeros((64 * depth, width), jnp.float32)
    for tap in range(27):
        a, b, c = (tap // 9, tap // 3 % 3, tap % 3)
        window = padded[a : a + 8, b : b + 8, c : c + depth].reshape(-1, width)
        total = total + jnp.dot(window, weight[tap], preferred_element_type=jnp.float32)
    return total


def weight_terms(padded, grad_flat, depth, width):
    terms = []
    for tap in range(27):
        a, b, c = (tap // 9, tap // 3 % 3, tap % 3)
        window = padded[a : a + 8, b : b + 8, c : c + depth].reshape(-1, width)
        terms.append(
            lax.dot_general(
                window, grad_flat, (((0,), (0,)), ((), ())), preferred_element_type=jnp.float32
            )
        )
    return jnp.stack(terms)


def backward_taps(padded, weight, depth, width):
    total = jnp.zeros((64 * depth, width), jnp.float32)
    for tap in range(27):
        a, b, c = (tap // 9, tap // 3 % 3, tap % 3)
        window = padded[2 - a : 10 - a, 2 - b : 10 - b, 2 - c : 2 - c + depth].reshape(-1, width)
        total = total + jnp.dot(window, weight[tap].T, preferred_element_type=jnp.float32)
    return total


def on_device(points, counts, voxels, occupancy, weight, w_in, cotangent):
    width = weight.shape[2]
    feat_width = points.shape[4]
    depth = cotangent.shape[2]
    shape_slots = voxels.shape
    slots = lax.broadcasted_iota(jnp.int32, shape_slots, 3)
    got_points, got_voxels, got_counts = (
        lax.all_to_all(points, "gx", split_axis=2, concat_axis=2, tiled=True),
        lax.all_to_all(voxels, "gx", split_axis=2, concat_axis=2, tiled=True),
        lax.all_to_all(counts, "gx", split_axis=2, concat_axis=2, tiled=True),
    )
    got_valid = (slots < got_counts[..., None]).astype(jnp.float32).reshape(-1, 1)
    proj = (
        jnp.dot(got_points.reshape(-1, feat_width), w_in, preferred_element_type=jnp.float32)
        * got_valid
    ).astype(jnp.bfloat16)
    flat_index = got_voxels.reshape(-1)
    column_mask = jnp.repeat(occupancy[0, 0], 8).astype(jnp.float32)
    mask = jnp.broadcast_to(column_mask[None, None, :, None], (8, 8, depth, 1))
    summed = (
        jnp.zeros((64 * depth, width), jnp.float32).at[flat_index].add(proj.astype(jnp.float32))
    )
    feature = (summed.reshape(8, 8, depth, width) * mask).astype(jnp.bfloat16)
    grad_masked = (cotangent.astype(jnp.float32) * mask).astype(jnp.bfloat16)
    feature_pad = pad_depth(padded_2(feature, (("gx", 0), ("gy", 1)), 1))
    grad_pad = pad_depth(padded_2(grad_masked, (("gx", 0), ("gy", 1)), 1))
    mask_flat = mask.reshape(-1, 1)
    output = (forward_taps(feature_pad, weight, depth, width) * mask_flat).astype(jnp.bfloat16)
    local_grad = weight_terms(feature_pad, grad_masked.reshape(-1, width), depth, width)
    weight_grad = lax.psum(local_grad, ("gx", "gy"))
    feature_grad = (backward_taps(grad_pad, weight, depth, width) * mask_flat).astype(jnp.bfloat16)
    out_rows = (output[flat_index].astype(jnp.float32) * got_valid).astype(jnp.bfloat16)
    grad_rows = feature_grad[flat_index]
    point_rows = jnp.dot(grad_rows, w_in.T, preferred_element_type=jnp.float32) * got_valid
    sent_point = point_rows.astype(jnp.bfloat16).reshape(shape_slots + (feat_width,))
    point_feat, point_grad = (
        lax.all_to_all(
            out_rows.reshape(shape_slots + (width,)), "gx", split_axis=2, concat_axis=2, tiled=True
        ),
        lax.all_to_all(sent_point, "gx", split_axis=2, concat_axis=2, tiled=True),
    )
    return (point_feat, point_grad, weight_grad)


def solution(mesh):
    placed = (
        P("gy", "gx", None, None, None),
        P("gy", "gx", None),
        P("gy", "gx", None, None),
        P("gx", "gy", None),
        P(),
        P(),
        P("gx", "gy", None, None),
    )
    return jax.shard_map(
        on_device,
        mesh=mesh,
        in_specs=placed,
        out_specs=(P("gy", "gx", None, None, None), P("gy", "gx", None, None, None), P()),
        check_vma=False,
    )
```

profile of v0, /device:TPU:1, one launch (start us, length us, event | category | flops | bytes accessed | tf_op | source)
XLA Modules:
  0.0 468.1 jit_solution(846735209724311216)
XLA Ops:
  7.2 1.4 copy.31
  8.5 15.1 %all-to-all-start.2 = ((s32[1,1,64]{1,0,2:T(1,128)}), s32[1,1,64]{1,0,2:T(1,128)S(1)}, u32[]{:S(2)}, u32[]{:S(2)}) async-start(s32[1,1,64]{1,0,2:T(1,128)} %copy.31), calls=%async_computation.2 | async-start | bytes 65536 | tf_op jit(solution)/shard_map/all_to_all | solution.py:64
  23.7 1.4 copy.29
  25.1 9.3 %all-to-all-done.2 = s32[1,1,64]{1,0,2:T(1,128)S(1)} async-done(((s32[1,1,64]{1,0,2:T(1,128)}), s32[1,1,64]{1,0,2:T(1,128)S(1)}, u32[]{:S(2)}, u32[]{:S(2)}) %all-to-all-start.2) | async-done | bytes 288 | tf_op jit(solution)/shard_map/all_to_all | solution.py:64
  34.4 4.6 all-to-all-start
  39.0 0.7 convert_bitcast_fusion
  40.0 1.2 reduce.1
  41.4 8.4 %all-to-all-done = s32[1,1,64,32]{3,1,0,2:T(1,128)S(1)} async-done(((s32[1,1,64,32]{3,1,0,2:T(1,128)}), s32[1,1,64,32]{3,1,0,2:T(1,128)S(1)}, u32[]{:S(2)}, u32[]{:S(2)}) %all-to-all-start) | async-done | bytes 8224 | tf_op jit(solution)/shard_map/all_to_all | solution.py:63
  49.8 4.6 all-to-all-start.1
  54.5 0.5 broadcast.138
  55.0 0.7 reduce.4
  55.9 13.2 %all-to-all-done.1 = bf16[1,1,64,32,128]{4,3,1,0,2:T(8,128)(2,1)S(1)} async-done(((bf16[1,1,64,32,128]{4,3,1,0,2:T(8,128)(2,1)}), bf16[1,1,64,32,128]{4,3,1,0,2:T(8,128)(2,1)S(1)}, u32[]{:S(2)}, u32[]{:S(2)}) %all-to-all-start.1) | async-done | bytes 524320 | tf_op jit(solution)/shard_map/all_to_all | solution.py:62
  69.8 11.6 %scatter_custom_fusion = f32[1024,96]{1,0:T(8,128)S(1)} fusion(s32[2048]{0:T(1024)S(1)} %bitcast.568, f32[2048,96]{1,0:T(8,128)S(1)} %copy.32, f32[]{:T(128)} %constant.1.clone.1), kind=kCustom, calls=%fused_computation.151 | custom fusion | flops 196608 | bytes 393220 | tf_op jit(solution)/shard_map/scatter-add | solution.py:75
  81.6 1.3 collective-permute-start.1
  82.9 5.5 %collective-permute-start = (bf16[1,8,16,96]{3,2,1,0:T(8,128)(2,1)S(1)}, bf16[1,8,16,96]{3,2,1,0:T(8,128)(2,1)S(1)}, u32[]{:S(2)}, u32[]{:S(2)}) collective-permute-start(bf16[1,8,16,96]{3,2,1,0:T(8,128)(2,1)S(1)} %get-tuple-element.71), channel_id=1, source_target_pairs={{0,4},{4,8},{8,12},{12,16},{16,20},{20,24},{24,28},{28,32},{32,36}... | collective-permute-start | bytes 73736 | tf_op jit(solution)/shard_map/ppermute | solution.py:12
  88.6 1.3 collective-permute-start.5
  89.9 5.5 %collective-permute-start.4 = (bf16[1,8,16,96]{3,2,1,0:T(8,128)(2,1)S(1)}, bf16[1,8,16,96]{3,2,1,0:T(8,128)(2,1)S(1)}, u32[]{:S(2)}, u32[]{:S(2)}) collective-permute-start(bf16[1,8,16,96]{3,2,1,0:T(8,128)(2,1)S(1)} %get-tuple-element.67), channel_id=1, source_target_pairs={{0,4},{4,8},{8,12},{12,16},{16,20},{20,24},{24,28},{28,32},{32,36}... | collective-permute-start | bytes 73736 | tf_op jit(solution)/shard_map/ppermute | solution.py:12
  95.4 8.8 %collective-permute-start.3 = (bf16[10,1,16,96]{3,2,1,0:T(8,128)(2,1)S(1)}, bf16[10,1,16,96]{3,2,1,0:T(8,128)(2,1)S(1)}, u32[]{:S(2)}, u32[]{:S(2)}) collective-permute-start(bf16[10,1,16,96]{3,2,1,0:T(8,128)(2,1)S(1)} %get-tuple-element.64), channel_id=1, source_target_pairs={{1,0},{2,1},{3,2},{5,4},{6,5},{7,6},{9,8},{10,9},{11,10},{13,12},{... | collective-permute-start | bytes 92168 | tf_op jit(solution)/shard_map/ppermute | solution.py:15
  104.2 2.1 collective-permute-start.2
  106.4 0.6 pad_maximum_fusion.8
  107.0 2.2 collective-permute-start.7
  109.2 3.5 collective-permute-start.6
  113.3 1.1 fusion.190
  115.3 0.4 fusion.193
  122.1 6.2 %gather_fusion = bf16[2048,96]{1,0:T(8,128)(2,1)S(1)} fusion(bf16[1024,96]{1,0:T(8,128)(2,1)S(1)} %copy.34, s32[2048]{0:T(1024)S(1)} %broadcast_clamp_fusion), kind=kCustom, calls=%fused_computation | custom fusion | bytes 794624 | tf_op jit(solution)/shard_map/gather | solution.py:86
  128.3 1.1 fusion.39
  129.4 0.9 fusion.38
  130.3 14.4 %all-to-all-start.3 = ((bf16[1,1,64,32,96]{4,3,1,0,2:T(8,128)(2,1)}), bf16[1,1,64,32,96]{4,3,1,0,2:T(8,128)(2,1)S(1)}, u32[]{:S(2)}, u32[]{:S(2)}) async-start(bf16[1,1,64,32,96]{4,3,1,0,2:T(8,128)(2,1)} %fusion.39), calls=%async_computation.3 | async-start | bytes 1048576 | tf_op jit(solution)/shard_map/all_to_all | solution.py:91
  145.0 1.1 fusion.189
  146.8 0.9 fusion.19
  147.7 0.9 fusion.37
  148.6 0.9 fusion.36
  149.4 0.9 fusion.18
  150.3 0.9 fusion.35
  151.2 0.9 fusion.34
  152.1 0.9 fusion.17
  152.9 0.9 fusion.33
  153.8 0.9 fusion.32
  154.7 0.9 fusion.16
  155.6 0.9 fusion.31
  156.4 0.9 fusion.30
  157.3 0.9 fusion.29
  158.2 0.9 fusion.28
  159.1 0.9 fusion.27
  159.9 0.9 fusion.15
  160.8 0.9 fusion.26
  161.7 0.9 fusion.25
  162.6 0.9 fusion.14
  163.4 0.9 fusion.24
  164.4 0.4 fusion.191
  170.3 0.9 fusion.23
  171.3 6.2 %gather_fusion.1 = bf16[2048,96]{1,0:T(8,128)(2,1)S(1)} fusion(bf16[1024,96]{1,0:T(8,128)(2,1)S(1)} %copy.36, s32[2048]{0:T(1024)S(1)} %broadcast_clamp_fusion), kind=kCustom, calls=%fused_computation.1 | custom fusion | bytes 794624 | tf_op jit(solution)/shard_map/gather | solution.py:87
  177.5 0.9 fusion.13
  178.4 0.9 fusion.22
  179.3 1.2 fusion
  180.4 11.9 %all-to-all-start.4 = ((bf16[1,1,64,32,128]{4,3,1,0,2:T(8,128)(2,1)}), bf16[1,1,64,32,128]{4,3,1,0,2:T(8,128)(2,1)S(1)}, u32[]{:S(2)}, u32[]{:S(2)}) async-start(bf16[1,1,64,32,128]{4,3,1,0,2:T(8,128)(2,1)} %bitcast.89), calls=%async_computation.4 | async-start | bytes 1048576 | tf_op jit(solution)/shard_map/all_to_all | solution.py:94
  192.4 0.9 fusion.21
  193.3 0.9 fusion.12
  194.2 0.9 fusion.20
  195.1 16.9 %all-to-all-done.4 = bf16[1,1,64,32,128]{4,3,1,0,2:T(8,128)(2,1)S(1)} async-done(((bf16[1,1,64,32,128]{4,3,1,0,2:T(8,128)(2,1)}), bf16[1,1,64,32,128]{4,3,1,0,2:T(8,128)(2,1)S(1)}, u32[]{:S(2)}, u32[]{:S(2)}) %all-to-all-start.4) | async-done | bytes 524320 | tf_op jit(solution)/shard_map/all_to_all | solution.py:94
  211.9 246.7 %all-reduce.4.cloned.1.call-done = f32[27,96,96]{2,1,0:T(8,128)} async-done(((f32[27,96,96]{2,1,0:T(8,128)}), f32[27,96,96]{2,1,0:T(8,128)}) %all-reduce.4.cloned.1.call-update) | async-done | bytes 995344 | tf_op jit(solution)/shard_map/psum | solution.py:84
  458.6 0.8 copy.96
  459.4 0.8 copy.97
  460.2 1.1 copy.98
  (101 shorter events, 16.1 us)
Async XLA Ops:
  7.2 61.9 %copy-start = (bf16[128,96]{0,1:T(8,128)(2,1)S(1)}, bf16[128,96]{0,1:T(8,128)(2,1)}, u32[]{:S(2)}) copy-start(bf16[128,96]{0,1:T(8,128)(2,1)} %param.12) | copy-start | bytes 73732
  8.5 25.9 %all-to-all-start.2 = ((s32[1,1,64]{1,0,2:T(1,128)}), s32[1,1,64]{1,0,2:T(1,128)S(1)}, u32[]{:S(2)}, u32[]{:S(2)}) async-start(s32[1,1,64]{1,0,2:T(1,128)} %copy.31), calls=%async_computation.2 | async-start | bytes 65536 | tf_op jit(solution)/shard_map/all_to_all | solution.py:64
  34.4 15.4 %all-to-all-start = ((s32[1,1,64,32]{3,1,0,2:T(1,128)}), s32[1,1,64,32]{3,1,0,2:T(1,128)S(1)}, u32[]{:S(2)}, u32[]{:S(2)}) async-start(s32[1,1,64,32]{3,1,0,2:T(1,128)} %copy.29), calls=%async_computation | async-start | bytes 65536 | tf_op jit(solution)/shard_map/all_to_all | solution.py:63
  49.8 19.3 %all-to-all-start.1 = ((bf16[1,1,64,32,128]{4,3,1,0,2:T(8,128)(2,1)}), bf16[1,1,64,32,128]{4,3,1,0,2:T(8,128)(2,1)S(1)}, u32[]{:S(2)}, u32[]{:S(2)}) async-start(bf16[1,1,64,32,128]{4,3,1,0,2:T(8,128)(2,1)} %bitcast.566), calls=%async_computation.1 | async-start | bytes 1048576 | tf_op jit(solution)/shard_map/all_to_all | solution.py:62
  69.4 12.0 %copy-start.3 = (bf16[8,8,16,96]{3,2,1,0:T(8,128)(2,1)S(1)}, bf16[8,8,16,96]{3,2,1,0:T(8,128)(2,1)}, u32[]{:S(2)}) copy-start(bf16[8,8,16,96]{3,2,1,0:T(8,128)(2,1)} %param.13) | copy-start | bytes 589828
  81.6 13.8 %collective-permute-start.1 = (bf16[1,8,16,96]{3,2,1,0:T(8,128)(2,1)S(1)}, bf16[1,8,16,96]{3,2,1,0:T(8,128)(2,1)S(1)}, u32[]{:S(2)}, u32[]{:S(2)}) collective-permute-start(bf16[1,8,16,96]{3,2,1,0:T(8,128)(2,1)S(1)} %get-tuple-element.72), channel_id=1, source_target_pairs={{4,0},{8,4},{12,8},{16,12},{20,16},{24,20},{28,24},{32,28},{36,32}... | collective-permute-start | bytes 73736 | tf_op jit(solution)/shard_map/ppermute | solution.py:15
  82.9 12.5 %collective-permute-start = (bf16[1,8,16,96]{3,2,1,0:T(8,128)(2,1)S(1)}, bf16[1,8,16,96]{3,2,1,0:T(8,128)(2,1)S(1)}, u32[]{:S(2)}, u32[]{:S(2)}) collective-permute-start(bf16[1,8,16,96]{3,2,1,0:T(8,128)(2,1)S(1)} %get-tuple-element.71), channel_id=1, source_target_pairs={{0,4},{4,8},{8,12},{12,16},{16,20},{20,24},{24,28},{28,32},{32,36}... | collective-permute-start | bytes 73736 | tf_op jit(solution)/shard_map/ppermute | solution.py:12
  88.6 17.8 %collective-permute-start.5 = (bf16[1,8,16,96]{3,2,1,0:T(8,128)(2,1)S(1)}, bf16[1,8,16,96]{3,2,1,0:T(8,128)(2,1)S(1)}, u32[]{:S(2)}, u32[]{:S(2)}) collective-permute-start(bf16[1,8,16,96]{3,2,1,0:T(8,128)(2,1)S(1)} %get-tuple-element.68), channel_id=1, source_target_pairs={{4,0},{8,4},{12,8},{16,12},{20,16},{24,20},{28,24},{32,28},{36,32}... | collective-permute-start | bytes 73736 | tf_op jit(solution)/shard_map/ppermute | solution.py:15
  89.9 16.5 %collective-permute-start.4 = (bf16[1,8,16,96]{3,2,1,0:T(8,128)(2,1)S(1)}, bf16[1,8,16,96]{3,2,1,0:T(8,128)(2,1)S(1)}, u32[]{:S(2)}, u32[]{:S(2)}) collective-permute-start(bf16[1,8,16,96]{3,2,1,0:T(8,128)(2,1)S(1)} %get-tuple-element.67), channel_id=1, source_target_pairs={{0,4},{4,8},{8,12},{12,16},{16,20},{20,24},{24,28},{28,32},{32,36}... | collective-permute-start | bytes 73736 | tf_op jit(solution)/shard_map/ppermute | solution.py:12
  95.4 17.5 %collective-permute-start.3 = (bf16[10,1,16,96]{3,2,1,0:T(8,128)(2,1)S(1)}, bf16[10,1,16,96]{3,2,1,0:T(8,128)(2,1)S(1)}, u32[]{:S(2)}, u32[]{:S(2)}) collective-permute-start(bf16[10,1,16,96]{3,2,1,0:T(8,128)(2,1)S(1)} %get-tuple-element.64), channel_id=1, source_target_pairs={{1,0},{2,1},{3,2},{5,4},{6,5},{7,6},{9,8},{10,9},{11,10},{13,12},{... | collective-permute-start | bytes 92168 | tf_op jit(solution)/shard_map/ppermute | solution.py:15
  104.2 8.7 %collective-permute-start.2 = (bf16[10,1,16,96]{3,2,1,0:T(8,128)(2,1)S(1)}, bf16[10,1,16,96]{3,2,1,0:T(8,128)(2,1)S(1)}, u32[]{:S(2)}, u32[]{:S(2)}) collective-permute-start(bf16[10,1,16,96]{3,2,1,0:T(8,128)(2,1)S(1)} %get-tuple-element.63), channel_id=1, source_target_pairs={{0,1},{1,2},{2,3},{4,5},{5,6},{6,7},{8,9},{9,10},{10,11},{12,13},{... | collective-permute-start | bytes 92168 | tf_op jit(solution)/shard_map/ppermute | solution.py:12
  107.0 37.7 %collective-permute-start.7 = (bf16[10,1,16,96]{3,2,1,0:T(8,128)(2,1)}, bf16[10,1,16,96]{3,2,1,0:T(8,128)(2,1)S(1)}, u32[]{:S(2)}, u32[]{:S(2)}) collective-permute-start(bf16[10,1,16,96]{3,2,1,0:T(8,128)(2,1)} %get-tuple-element.60), channel_id=1, source_target_pairs={{1,0},{2,1},{3,2},{5,4},{6,5},{7,6},{9,8},{10,9},{11,10},{13,12},{... | collective-permute-start | bytes 92168 | tf_op jit(solution)/shard_map/ppermute | solution.py:15
  109.2 35.5 %collective-permute-start.6 = (bf16[10,1,16,96]{3,2,1,0:T(8,128)(2,1)S(1)}, bf16[10,1,16,96]{3,2,1,0:T(8,128)(2,1)S(1)}, u32[]{:S(2)}, u32[]{:S(2)}) collective-permute-start(bf16[10,1,16,96]{3,2,1,0:T(8,128)(2,1)S(1)} %get-tuple-element.59), channel_id=1, source_target_pairs={{0,1},{1,2},{2,3},{4,5},{5,6},{6,7},{8,9},{9,10},{10,11},{12,13},{... | collective-permute-start | bytes 92168 | tf_op jit(solution)/shard_map/ppermute | solution.py:12
  113.3 1.1 copy-start.1
  130.3 50.1 %all-to-all-start.3 = ((bf16[1,1,64,32,96]{4,3,1,0,2:T(8,128)(2,1)}), bf16[1,1,64,32,96]{4,3,1,0,2:T(8,128)(2,1)S(1)}, u32[]{:S(2)}, u32[]{:S(2)}) async-start(bf16[1,1,64,32,96]{4,3,1,0,2:T(8,128)(2,1)} %fusion.39), calls=%async_computation.3 | async-start | bytes 1048576 | tf_op jit(solution)/shard_map/all_to_all | solution.py:91
  180.4 31.5 %all-to-all-start.4 = ((bf16[1,1,64,32,128]{4,3,1,0,2:T(8,128)(2,1)}), bf16[1,1,64,32,128]{4,3,1,0,2:T(8,128)(2,1)S(1)}, u32[]{:S(2)}, u32[]{:S(2)}) async-start(bf16[1,1,64,32,128]{4,3,1,0,2:T(8,128)(2,1)} %bitcast.89), calls=%async_computation.4 | async-start | bytes 1048576 | tf_op jit(solution)/shard_map/all_to_all | solution.py:94
  192.4 266.3 %all-reduce.4.cloned.1.call-start = ((), (), s32[]{:S(2)}) async-start(), calls=%async_computation.5 | async-start | bytes 2654208 | tf_op jit(solution)/shard_map/psum | solution.py:84
  458.6 1.6 copy-start.2
Sparse Core Ops, SparseCore 0:
  199.2 259.4 all-reduce.3
where the time goes:
time: 469 us; the launch traced here: 468 us
  waiting for transfers between devices  295 us (63%)
  starting transfers between devices  80.9 us (17%)
  matrix products  38.1 us (8%)
  local copies, waits for them, and re-layouts  22.7 us (5%)
  other arithmetic  17.2 us (4%)
  between operations  14.6 us (3%)
    psum x1, waiting for transfers between devices, on_device(): weight_grad = lax.psum(local_grad, ('gx', 'gy'))  247 us
    dot_general x27, matrix products, weight_terms(): lax.dot_general(window, grad_flat, (((0,), (0,)), ((), ())), preferred_el...  23.6 us
    all_to_all x1, waiting for transfers between devices, on_device(): lax.all_to_all(sent_point, 'gx', split_axis=2, concat_axis=2, tiled=True)  16.9 us
    ppermute x4, starting transfers between devices, padded_2(): lax.ppermute(lax.slice_in_dim(block, block.shape[dim] - width, None, axis...  16.6 us
    all_to_all x1, starting transfers between devices, on_device(): lax.all_to_all(counts, 'gx', split_axis=2, concat_axis=2, tiled=True)  15.1 us
    all_to_all x1, starting transfers between devices, on_device(): lax.all_to_all(out_rows.reshape(shape_slots + (width,)), 'gx', split_axis...  14.4 us
    ppermute x4, starting transfers between devices, padded_2(): lax.ppermute(lax.slice_in_dim(block, 0, width, axis=dim), axis, backward)  13.6 us
    all_to_all x1, waiting for transfers between devices, on_device(): lax.all_to_all(points, 'gx', split_axis=2, concat_axis=2, tiled=True)  13.2 us
  transfers between devices with their start and end apart: 14, of which 5 were waited for; matrix products, arithmetic and copies ran while one was open for 13% of the time, Pallas kernels for 0%

commit v1 on v0

--- a/solution.py
+++ b/solution.py
@@ -81,7 +81,7 @@
     mask_flat = mask.reshape(-1, 1)
     output = (forward_taps(feature_pad, weight, depth, width) * mask_flat).astype(jnp.bfloat16)
     local_grad = weight_terms(feature_pad, grad_masked.reshape(-1, width), depth, width)
-    weight_grad = lax.psum(local_grad, ("gx", "gy"))
+    weight_grad = lax.psum(lax.psum(local_grad, "gx"), "gy")
     feature_grad = (backward_taps(grad_pad, weight, depth, width) * mask_flat).astype(jnp.bfloat16)
     out_rows = (output[flat_index].astype(jnp.float32) * got_valid).astype(jnp.bfloat16)
     grad_rows = feature_grad[flat_index]

time: 469 us -> 921 us (1.96)
  waiting for transfers between devices: 295 us -> 740 us
    psum x1 -> x2, waiting for transfers between devices: 247 us -> 709 us  [on_device(): weight_grad = lax.psum(lax.psum(local_grad, 'gx'), 'gy')]
    all_to_all x1, waiting for transfers between devices: 16.9 us -> 0.01 us  [on_device(): lax.all_to_all(sent_point, 'gx', split_axis=2, concat_axis=2, tiled=True)]
  transfers between devices with their start and end apart: 14 -> 15, of which waited for: 5 -> 5; matrix products, arithmetic and copies ran while one was open for 13% -> 7% of each run, Pallas kernels for 0% -> 0%
where the time goes in v1:
time: 921 us; the launch traced here: 920 us
  waiting for transfers between devices  740 us (80%)
  starting transfers between devices  81.2 us (9%)
  matrix products  38.8 us (4%)
  local copies, waits for them, and re-layouts  27.5 us (3%)
  other arithmetic  17.4 us (2%)
  between operations  14.7 us (2%)
    psum x2, waiting for transfers between devices, on_device(): weight_grad = lax.psum(lax.psum(local_grad, 'gx'), 'gy')  709 us
    dot_general x27, matrix products, weight_terms(): lax.dot_general(window, grad_flat, (((0,), (0,)), ((), ())), preferred_el...  23.6 us
  transfers between devices with their start and end apart: 15, of which 5 were waited for; matrix products, arithmetic and copies ran while one was open for 7% of the time, Pallas kernels for 0%

profile of v1, /device:TPU:1, one launch (start us, length us, event | category | flops | bytes accessed | tf_op | source)
XLA Modules:
  0.0 920.0 jit_solution(17451816771303071328)
XLA Ops:
  7.2 1.4 copy.31
  8.5 15.1 %all-to-all-start.2 = ((s32[1,1,64]{1,0,2:T(1,128)}), s32[1,1,64]{1,0,2:T(1,128)S(1)}, u32[]{:S(2)}, u32[]{:S(2)}) async-start(s32[1,1,64]{1,0,2:T(1,128)} %copy.31), calls=%async_computation.2 | async-start | bytes 65536 | tf_op jit(solution)/shard_map/all_to_all | solution.py:64
  23.7 1.4 copy.29
  25.1 9.3 %all-to-all-done.2 = s32[1,1,64]{1,0,2:T(1,128)S(1)} async-done(((s32[1,1,64]{1,0,2:T(1,128)}), s32[1,1,64]{1,0,2:T(1,128)S(1)}, u32[]{:S(2)}, u32[]{:S(2)}) %all-to-all-start.2) | async-done | bytes 288 | tf_op jit(solution)/shard_map/all_to_all | solution.py:64
  34.4 4.6 all-to-all-start
  39.0 0.7 convert_bitcast_fusion
  40.0 1.2 reduce.1
  41.4 8.4 all-to-all-done
  49.8 4.6 all-to-all-start.1
  54.5 0.5 broadcast.138
  55.0 0.7 reduce.4
  55.9 13.2 %all-to-all-done.1 = bf16[1,1,64,32,128]{4,3,1,0,2:T(8,128)(2,1)S(1)} async-done(((bf16[1,1,64,32,128]{4,3,1,0,2:T(8,128)(2,1)}), bf16[1,1,64,32,128]{4,3,1,0,2:T(8,128)(2,1)S(1)}, u32[]{:S(2)}, u32[]{:S(2)}) %all-to-all-start.1) | async-done | bytes 524320 | tf_op jit(solution)/shard_map/all_to_all | solution.py:62
  69.8 11.6 %scatter_custom_fusion = f32[1024,96]{1,0:T(8,128)S(1)} fusion(s32[2048]{0:T(1024)S(1)} %bitcast.568, f32[2048,96]{1,0:T(8,128)S(1)} %copy.32, f32[]{:T(128)} %constant.1.clone.1), kind=kCustom, calls=%fused_computation.151 | custom fusion | flops 196608 | bytes 393220 | tf_op jit(solution)/shard_map/scatter-add | solution.py:75
  81.6 1.3 collective-permute-start.1
  82.9 5.5 collective-permute-start
  88.6 1.3 collective-permute-start.5
  89.9 5.5 collective-permute-start.4
  95.4 8.8 collective-permute-start.3
  104.2 2.1 collective-permute-start.2
  106.4 2.2 collective-permute-start.7
  108.6 3.5 collective-permute-start.6
  112.3 0.9 pad_maximum_fusion.2
  113.4 1.1 fusion.190
  122.3 6.2 gather_fusion
  128.5 1.1 fusion.39
  129.6 0.9 fusion.38
  130.5 14.2 %all-to-all-start.3 = ((bf16[1,1,64,32,96]{4,3,1,0,2:T(8,128)(2,1)}), bf16[1,1,64,32,96]{4,3,1,0,2:T(8,128)(2,1)S(1)}, u32[]{:S(2)}, u32[]{:S(2)}) async-start(bf16[1,1,64,32,96]{4,3,1,0,2:T(8,128)(2,1)} %fusion.39), calls=%async_computation.3 | async-start | bytes 1048576 | tf_op jit(solution)/shard_map/all_to_all | solution.py:91
  145.3 2.0 fusion.189
  147.5 1.0 fusion.99
  148.7 0.9 fusion.19
  149.6 0.9 fusion.37
  150.5 0.9 fusion.36
  151.3 0.9 fusion.18
  152.2 0.9 fusion.35
  153.1 0.9 fusion.34
  153.9 0.9 fusion.17
  154.8 0.9 fusion.33
  155.7 0.9 fusion.32
  156.6 0.9 fusion.16
  157.4 0.9 fusion.31
  158.3 0.9 fusion.30
  159.2 0.9 fusion.29
  160.1 0.9 fusion.28
  160.9 0.9 fusion.27
  161.8 0.9 fusion.15
  162.7 0.9 fusion.26
  163.6 0.9 fusion.25
  164.4 0.9 fusion.14
  165.3 0.9 fusion.24
  166.2 0.9 fusion.23
  167.1 0.9 fusion.13
  167.9 0.9 fusion.22
  168.8 0.9 fusion.21
  169.7 0.9 fusion.12
  170.6 0.9 fusion.20
  172.1 0.4 copy-done.18
  181.6 6.2 gather_fusion.1
  187.8 1.2 fusion
  189.0 12.1 %all-to-all-start.4 = ((bf16[1,1,64,32,128]{4,3,1,0,2:T(8,128)(2,1)}), bf16[1,1,64,32,128]{4,3,1,0,2:T(8,128)(2,1)S(1)}, u32[]{:S(2)}, u32[]{:S(2)}) async-start(bf16[1,1,64,32,128]{4,3,1,0,2:T(8,128)(2,1)} %bitcast.89), calls=%async_computation.4 | async-start | bytes 1048576 | tf_op jit(solution)/shard_map/all_to_all | solution.py:94
  201.2 618.4 %all-reduce.5.cloned.1.call-done = f32[27,96,96]{2,1,0:T(8,128)} async-done(((f32[27,96,96]{2,1,0:T(8,128)}), f32[27,96,96]{2,1,0:T(8,128)}) %all-reduce.5.cloned.1.call-update) | async-done | bytes 995344 | tf_op jit(solution)/shard_map/psum | solution.py:84
  819.6 90.9 %all-reduce.7.cloned.1.call-done = f32[27,96,96]{2,1,0:T(8,128)} async-done(((f32[27,96,96]{2,1,0:T(8,128)}), f32[27,96,96]{2,1,0:T(8,128)}) %all-reduce.7.cloned.1.call-update) | async-done | bytes 995344 | tf_op jit(solution)/shard_map/psum | solution.py:84
  910.5 0.8 copy.97
  911.3 0.8 copy.98
  912.1 1.1 copy.99
  (140 shorter events, 20.4 us)
Async XLA Ops:
  7.2 61.9 %copy-start = (bf16[128,96]{0,1:T(8,128)(2,1)S(1)}, bf16[128,96]{0,1:T(8,128)(2,1)}, u32[]{:S(2)}) copy-start(bf16[128,96]{0,1:T(8,128)(2,1)} %param.12) | copy-start | bytes 73732
  8.5 25.9 %all-to-all-start.2 = ((s32[1,1,64]{1,0,2:T(1,128)}), s32[1,1,64]{1,0,2:T(1,128)S(1)}, u32[]{:S(2)}, u32[]{:S(2)}) async-start(s32[1,1,64]{1,0,2:T(1,128)} %copy.31), calls=%async_computation.2 | async-start | bytes 65536 | tf_op jit(solution)/shard_map/all_to_all | solution.py:64
  34.4 15.4 %all-to-all-start = ((s32[1,1,64,32]{3,1,0,2:T(1,128)}), s32[1,1,64,32]{3,1,0,2:T(1,128)S(1)}, u32[]{:S(2)}, u32[]{:S(2)}) async-start(s32[1,1,64,32]{3,1,0,2:T(1,128)} %copy.29), calls=%async_computation | async-start | bytes 65536 | tf_op jit(solution)/shard_map/all_to_all | solution.py:63
  49.8 19.3 %all-to-all-start.1 = ((bf16[1,1,64,32,128]{4,3,1,0,2:T(8,128)(2,1)}), bf16[1,1,64,32,128]{4,3,1,0,2:T(8,128)(2,1)S(1)}, u32[]{:S(2)}, u32[]{:S(2)}) async-start(bf16[1,1,64,32,128]{4,3,1,0,2:T(8,128)(2,1)} %bitcast.566), calls=%async_computation.1 | async-start | bytes 1048576 | tf_op jit(solution)/shard_map/all_to_all | solution.py:62
  69.4 12.0 %copy-start.21 = (bf16[8,8,16,96]{3,2,1,0:T(8,128)(2,1)S(1)}, bf16[8,8,16,96]{3,2,1,0:T(8,128)(2,1)}, u32[]{:S(2)}) copy-start(bf16[8,8,16,96]{3,2,1,0:T(8,128)(2,1)} %param.13) | copy-start | bytes 589828
  81.6 13.8 %collective-permute-start.1 = (bf16[1,8,16,96]{3,2,1,0:T(8,128)(2,1)S(1)}, bf16[1,8,16,96]{3,2,1,0:T(8,128)(2,1)S(1)}, u32[]{:S(2)}, u32[]{:S(2)}) collective-permute-start(bf16[1,8,16,96]{3,2,1,0:T(8,128)(2,1)S(1)} %get-tuple-element.72), channel_id=1, source_target_pairs={{4,0},{8,4},{12,8},{16,12},{20,16},{24,20},{28,24},{32,28},{36,32}... | collective-permute-start | bytes 73736 | tf_op jit(solution)/shard_map/ppermute | solution.py:15
  82.9 12.5 %collective-permute-start = (bf16[1,8,16,96]{3,2,1,0:T(8,128)(2,1)S(1)}, bf16[1,8,16,96]{3,2,1,0:T(8,128)(2,1)S(1)}, u32[]{:S(2)}, u32[]{:S(2)}) collective-permute-start(bf16[1,8,16,96]{3,2,1,0:T(8,128)(2,1)S(1)} %get-tuple-element.71), channel_id=1, source_target_pairs={{0,4},{4,8},{8,12},{12,16},{16,20},{20,24},{24,28},{28,32},{32,36}... | collective-permute-start | bytes 73736 | tf_op jit(solution)/shard_map/ppermute | solution.py:12
  88.6 17.8 %collective-permute-start.5 = (bf16[1,8,16,96]{3,2,1,0:T(8,128)(2,1)S(1)}, bf16[1,8,16,96]{3,2,1,0:T(8,128)(2,1)S(1)}, u32[]{:S(2)}, u32[]{:S(2)}) collective-permute-start(bf16[1,8,16,96]{3,2,1,0:T(8,128)(2,1)S(1)} %get-tuple-element.68), channel_id=1, source_target_pairs={{4,0},{8,4},{12,8},{16,12},{20,16},{24,20},{28,24},{32,28},{36,32}... | collective-permute-start | bytes 73736 | tf_op jit(solution)/shard_map/ppermute | solution.py:15
  89.9 16.5 %collective-permute-start.4 = (bf16[1,8,16,96]{3,2,1,0:T(8,128)(2,1)S(1)}, bf16[1,8,16,96]{3,2,1,0:T(8,128)(2,1)S(1)}, u32[]{:S(2)}, u32[]{:S(2)}) collective-permute-start(bf16[1,8,16,96]{3,2,1,0:T(8,128)(2,1)S(1)} %get-tuple-element.67), channel_id=1, source_target_pairs={{0,4},{4,8},{8,12},{12,16},{16,20},{20,24},{24,28},{28,32},{32,36}... | collective-permute-start | bytes 73736 | tf_op jit(solution)/shard_map/ppermute | solution.py:12
  95.4 17.7 %collective-permute-start.3 = (bf16[10,1,16,96]{3,2,1,0:T(8,128)(2,1)S(1)}, bf16[10,1,16,96]{3,2,1,0:T(8,128)(2,1)S(1)}, u32[]{:S(2)}, u32[]{:S(2)}) collective-permute-start(bf16[10,1,16,96]{3,2,1,0:T(8,128)(2,1)S(1)} %get-tuple-element.64), channel_id=1, source_target_pairs={{1,0},{2,1},{3,2},{5,4},{6,5},{7,6},{9,8},{10,9},{11,10},{13,12},{... | collective-permute-start | bytes 92168 | tf_op jit(solution)/shard_map/ppermute | solution.py:15
  104.2 8.9 collective-permute-start.2
  106.4 38.5 %collective-permute-start.7 = (bf16[10,1,16,96]{3,2,1,0:T(8,128)(2,1)S(1)}, bf16[10,1,16,96]{3,2,1,0:T(8,128)(2,1)S(1)}, u32[]{:S(2)}, u32[]{:S(2)}) collective-permute-start(bf16[10,1,16,96]{3,2,1,0:T(8,128)(2,1)S(1)} %get-tuple-element.60), channel_id=1, source_target_pairs={{1,0},{2,1},{3,2},{5,4},{6,5},{7,6},{9,8},{10,9},{11,10},{13,12},{... | collective-permute-start | bytes 92168 | tf_op jit(solution)/shard_map/ppermute | solution.py:15
  108.6 36.3 %collective-permute-start.6 = (bf16[10,1,16,96]{3,2,1,0:T(8,128)(2,1)S(1)}, bf16[10,1,16,96]{3,2,1,0:T(8,128)(2,1)S(1)}, u32[]{:S(2)}, u32[]{:S(2)}) collective-permute-start(bf16[10,1,16,96]{3,2,1,0:T(8,128)(2,1)S(1)} %get-tuple-element.59), channel_id=1, source_target_pairs={{0,1},{1,2},{2,3},{4,5},{5,6},{6,7},{8,9},{9,10},{10,11},{12,13},{... | collective-permute-start | bytes 92168 | tf_op jit(solution)/shard_map/ppermute | solution.py:12
  113.4 1.1 copy-start.1
  130.5 58.5 %all-to-all-start.3 = ((bf16[1,1,64,32,96]{4,3,1,0,2:T(8,128)(2,1)}), bf16[1,1,64,32,96]{4,3,1,0,2:T(8,128)(2,1)S(1)}, u32[]{:S(2)}, u32[]{:S(2)}) async-start(bf16[1,1,64,32,96]{4,3,1,0,2:T(8,128)(2,1)} %fusion.39), calls=%async_computation.3 | async-start | bytes 1048576 | tf_op jit(solution)/shard_map/all_to_all | solution.py:91
  144.7 674.9 %all-reduce.5.cloned.1.call-start = ((), (), s32[]{:S(2)}) async-start(), calls=%async_computation.5 | async-start | bytes 2654208 | tf_op jit(solution)/shard_map/psum | solution.py:84
  171.6 1.0 copy-start.18
  171.9 1.0 copy-start.17
  172.1 1.0 copy-start.2
  172.1 1.1 copy-start.20
  172.8 1.0 copy-start.16
  173.4 1.0 copy-start.15
  174.0 1.0 copy-start.14
  174.6 1.0 copy-start.13
  175.2 1.0 copy-start.12
  175.8 1.0 copy-start.11
  176.4 1.0 copy-start.10
  177.0 1.0 copy-start.9
  177.6 1.0 copy-start.8
  178.2 1.0 copy-start.7
  178.8 1.0 copy-start.6
  179.0 1.0 copy-start.19
  179.4 1.0 copy-start.5
  180.2 1.0 copy-start.4
  189.0 630.6 %all-to-all-start.4 = ((bf16[1,1,64,32,128]{4,3,1,0,2:T(8,128)(2,1)}), bf16[1,1,64,32,128]{4,3,1,0,2:T(8,128)(2,1)S(1)}, u32[]{:S(2)}, u32[]{:S(2)}) async-start(bf16[1,1,64,32,128]{4,3,1,0,2:T(8,128)(2,1)} %bitcast.89), calls=%async_computation.4 | async-start | bytes 1048576 | tf_op jit(solution)/shard_map/all_to_all | solution.py:94
  201.1 709.4 %all-reduce.7.cloned.1.call-start = ((), (), s32[]{:S(2)}) async-start(), calls=%async_computation.6 | async-start | bytes 2654208 | tf_op jit(solution)/shard_map/psum | solution.py:84
  910.5 1.6 copy-start.3
Sparse Core Ops, SparseCore 0:
  171.6 647.9 all-reduce.4
  822.3 88.2 all-reduce.6
